TPU v7x, 256 devices: a whole 4x4x8 slice. The times are simulated.
256 devices in a mesh: tm: 8 (over y, core), vert: 32 (over z, x).
Axes of the slice: x: 4, y: 4, z: 8, core: 2. Of those that a mesh axis runs over, the one named last changes fastest.
Arguments:
- features: bfloat16 [32, 16384, 128], P('tm', 'vert'), may hold values from -6 to 6
- tile_cols: int32 [32, 128, 8], P('tm', 'vert'), may hold values from 0 to 127, as said below
- tile_vals: bfloat16 [32, 128, 8, 128, 128], P('tm', 'vert'), may hold values from -0.1875 to 0.1875
- space_weight: bfloat16 [128, 128], replicated, may hold values from -0.5 to 0.5
- positions: bfloat16 [32, 128], replicated, may hold values from -6 to 6
- attn_proj: bfloat16 [128, 384], replicated, may hold values from -0.5 to 0.5
- attn_out: bfloat16 [128, 128], replicated, may hold values from -0.5 to 0.5
- norm_gain: float32 [128], replicated, may hold values from 0.1 to 1.9
- mlp_up: bfloat16 [128, 512], replicated, may hold values from -0.5 to 0.5
- mlp_down: bfloat16 [512, 128], replicated, may hold values from -0.25 to 0.25
Outputs:
- embedded: bfloat16 [32, 16384, 128], P('tm', 'vert')
Inputs may be any that keep to these rules, and one draw needn't show every extreme that they name: `tile_cols`: for each snapshot and each group of 4 consecutive row blocks, the listed column blocks name at most two distinct blocks among those of any one group (blocks c with the same c // 4), and exactly two for some group.
All inputs are finite; a program needn't handle non-finite values.
Results may differ from a plain program's by a relative error of at most 0.0064.
Values may be sent and summed in bfloat16 or wider, within the bound.
A program may use at most 128 MiB of HBM per device.

v0:
```python
import math
import jax
import jax.numpy as jnp
from jax import lax
from jax.sharding import PartitionSpec as P

HEADS = 16
cap_value = 4.0
norm_eps = 1e-05


def temporal(hidden, positions, attn_proj, attn_out, norm_gain, mlp_up, mlp_down):
    snap_total = hidden.shape[0]
    feature_dim = hidden.shape[2]
    head_count = HEADS
    head_dim = feature_dim // head_count
    mixed_in = (hidden.astype(jnp.float32) + positions.astype(jnp.float32)[:, None, :]).astype(
        jnp.bfloat16
    )
    flat_in = mixed_in.reshape(-1, feature_dim)
    projected = jnp.dot(flat_in, attn_proj, preferred_element_type=jnp.float32).astype(jnp.bfloat16)
    projected = projected.reshape(snap_total, -1, 3, head_count, head_dim)
    query_part = projected[:, :, 0]
    key_part = projected[:, :, 1]
    value_part = projected[:, :, 2]
    scores = jnp.einsum(
        "tvhd,uvhd->vhtu", query_part, key_part, preferred_element_type=jnp.float32
    ) / math.sqrt(head_dim)
    capped = cap_value * jnp.tanh(scores / cap_value)
    causal = jnp.arange(snap_total)[:, None] >= jnp.arange(snap_total)[None, :]
    raised = jnp.where(causal, jnp.exp(capped), 0.0)
    weights = (raised / jnp.sum(raised, axis=-1, keepdims=True)).astype(jnp.bfloat16)
    attended = jnp.einsum(
        "vhtu,uvhd->tvhd", weights, value_part, preferred_element_type=jnp.float32
    ).astype(jnp.bfloat16)
    stream = flat_in.astype(jnp.float32) + jnp.dot(
        attended.reshape(-1, feature_dim), attn_out, preferred_element_type=jnp.float32
    )
    centre = jnp.mean(stream, axis=-1, keepdims=True)
    spread = jnp.mean((stream - centre) ** 2, axis=-1, keepdims=True)
    normed = ((stream - centre) * lax.rsqrt(spread + norm_eps) * norm_gain).astype(jnp.bfloat16)
    expanded = jax.nn.relu(jnp.dot(normed, mlp_up, preferred_element_type=jnp.float32)).astype(
        jnp.bfloat16
    )
    output = stream + jnp.dot(expanded, mlp_down, preferred_element_type=jnp.float32)
    return output.astype(jnp.bfloat16).reshape(snap_total, -1, feature_dim)


def spatial(features, tile_cols, tile_vals, space_weight):
    snap_count, row_count, feature_dim = features.shape
    tile_size = tile_vals.shape[-1]
    block_count = row_count // tile_size
    tile_count = tile_cols.shape[2]
    flat_cols = tile_cols.reshape(snap_count, block_count * tile_count)
    everything = lax.all_gather(features, "vert", axis=1, tiled=True)
    everything = everything.reshape(snap_count, -1, tile_size, feature_dim)
    blocks = jnp.take_along_axis(everything, flat_cols[:, :, None, None], axis=1)
    blocks = blocks.reshape(snap_count, block_count, tile_count, tile_size, feature_dim)
    summed = jnp.einsum(
        "srkij,srkjd->srid", tile_vals, blocks, preferred_element_type=jnp.float32
    ).astype(jnp.bfloat16)
    hidden = jax.nn.relu(
        jnp.dot(summed.reshape(-1, feature_dim), space_weight, preferred_element_type=jnp.float32)
    )
    return hidden.astype(jnp.bfloat16).reshape(snap_count, row_count, feature_dim)


def local(
    features,
    tile_cols,
    tile_vals,
    space_weight,
    positions,
    attn_proj,
    attn_out,
    norm_gain,
    mlp_up,
    mlp_down,
):
    snap_count, row_count, feature_dim = features.shape
    time_count = lax.axis_size("tm")
    hidden = spatial(features, tile_cols, tile_vals, space_weight)
    grouped = hidden.reshape(snap_count, time_count, row_count // time_count, feature_dim)
    arrived = lax.all_to_all(grouped, "tm", split_axis=1, concat_axis=0, tiled=True)
    snap_total = arrived.shape[0]
    timeline = arrived.reshape(snap_total, -1, feature_dim)
    result = temporal(timeline, positions, attn_proj, attn_out, norm_gain, mlp_up, mlp_down)
    result = result.reshape(snap_total, 1, -1, feature_dim)
    embedded = lax.all_to_all(result, "tm", split_axis=0, concat_axis=1, tiled=True)
    return embedded.reshape(snap_count, row_count, feature_dim)


def solution(mesh):
    placed = (
        P("tm", "vert", None),
        P("tm", "vert", None),
        P("tm", "vert", None, None, None),
        P(),
        P(),
        P(),
        P(),
        P(),
        P(),
        P(),
    )
    return jax.shard_map(
        local, mesh=mesh, in_specs=placed, out_specs=P("tm", "vert", None), check_vma=False
    )
```

profile of v0, /device:TPU:1, one launch (start us, length us, event | category | flops | bytes accessed | tf_op | source)
XLA Modules:
  0.0 253.4 jit_solution(15430646949209116984)
XLA Ops:
  6.5 0.0 copy-start
  6.5 0.0 all-gather.2.cloned.1.call-start
  6.5 0.7 all-gather.2.cloned.1.call-update
  7.3 0.8 broadcast_in_dim_reshape.3
  8.1 0.1 reshape.115
  8.1 0.7 compare_and_fusion
  8.8 143.9 %all-gather.2.cloned.1.call-done = bf16[4,16384,128]{2,1,0:T(8,128)(2,1)} async-done(((bf16[4,512,128]{2,1,0:T(8,128)(2,1)}), bf16[4,16384,128]{2,1,0:T(8,128)(2,1)}) %all-gather.2.cloned.1.call-update) | async-done | bytes 16777232 | tf_op jit(solution)/shard_map/all_gather | solution.py:55
  152.7 8.8 %gather_fusion = bf16[128,128,128]{2,1,0:T(8,128)(2,1)} fusion(bf16[4,128,128,128]{3,2,1,0:T(8,128)(2,1)} %bitcast.66, s32[128]{0:T(128)S(1)} %reshape.115), kind=kCustom, calls=%fused_computation | custom fusion | bytes 8389632 | tf_op jit(solution)/shard_map/jit(take_along_axis)/gather | solution.py:57
  161.6 0.0 copy-start.7
  161.6 0.0 copy-start.8
  161.6 4.8 %fusion.17 = bf16[4,4,128,128]{2,3,1,0:T(8,128)(2,1)S(1)} fusion(bf16[4,4,8,128,128]{4,3,2,1,0:T(8,128)(2,1)} %param.12, bf16[4,4,8,128,128]{4,3,2,1,0:T(8,128)(2,1)} %bitcast.63, pred[4,4,8]{2,1,0:T(4,128)(4,1)S(1)} %compare_and_fusion), kind=kOutput, calls=%fused_computation.22 | convolution fusion | flops 539230208 | bytes 8913024 | tf_op jit(solution)/shard_map/srkij,srkjd->srid/dot_general | solution.py:59
  166.4 0.0 copy-start.5
  166.4 0.0 copy-done.7
  166.4 0.3 fusion.5
  166.7 0.8 copy.25
  167.5 5.7 %all-to-all-start = ((bf16[4,8,64,128]{3,2,0,1:T(8,128)(2,1)}), bf16[4,8,64,128]{3,2,0,1:T(8,128)(2,1)S(1)}, u32[]{:S(2)}, u32[]{:S(2)}) async-start(bf16[4,8,64,128]{3,2,0,1:T(8,128)(2,1)} %copy.25), calls=%async_computation | async-start | bytes 1048576 | tf_op jit(solution)/shard_map/all_to_all | solution.py:84
  173.2 0.0 copy-done.8
  173.2 9.3 %all-to-all-done = bf16[4,8,64,128]{3,2,0,1:T(8,128)(2,1)S(1)} async-done(((bf16[4,8,64,128]{3,2,0,1:T(8,128)(2,1)}), bf16[4,8,64,128]{3,2,0,1:T(8,128)(2,1)S(1)}, u32[]{:S(2)}, u32[]{:S(2)}) %all-to-all-start) | async-done | bytes 524320 | tf_op jit(solution)/shard_map/all_to_all | solution.py:84
  182.6 0.1 bitcast_convert_fusion
  182.7 0.1 fusion.20
  182.8 0.0 copy-start.1
  182.8 0.8 copy-done.1
  183.5 0.0 copy-done.5
  183.6 0.5 convolution_convert_fusion
  184.1 1.7 copy.26
  185.8 4.6 %reshape.110 = bf16[32,64,3,16,8]{1,0,4,3,2:T(8,128)(2,1)S(1)} reshape(bf16[2048,384]{0,1:T(8,128)(2,1)} %copy.26) | data formatting | bytes 3145728 | tf_op jit(solution)/shard_map/reshape | solution.py:22
  190.4 1.8 fusion.35
  192.2 0.0 copy-start.3
  192.2 4.3 %copy.37 = bf16[32,64,1,16,8]{0,4,3,1,2:T(8,128)(2,1)S(1)} copy(bf16[32,64,1,16,8]{1,0,4,3,2:T(8,128)(2,1)} %get-tuple-element.6) | data formatting | bytes 1048576
  196.5 4.9 %copy.38 = bf16[32,64,1,16,8]{0,4,3,1,2:T(8,128)(2,1)} copy(bf16[32,64,1,16,8]{1,0,4,3,2:T(8,128)(2,1)} %get-tuple-element.7) | data formatting | bytes 1048576
  201.3 0.0 copy-done.3
  201.3 3.9 %copy.36 = bf16[32,64,1,16,8]{0,4,3,1,2:T(8,128)(2,1)} copy(bf16[32,64,1,16,8]{1,0,4,3,2:T(8,128)(2,1)S(1)} %copy-done.3) | data formatting | bytes 1048576
  205.2 0.0 copy-start.4
  205.2 11.1 %fusion = (f32[64,16,32]{2,1,0:T(8,128)S(1)}, f32[64,16,32,32]{2,3,1,0:T(8,128)}) fusion(pred[32,32]{0,1:T(8,128)(4,1)S(1)} %iota_compare_fusion, bf16[32,64,1,16,8]{0,4,3,1,2:T(8,128)(2,1)} %copy.38, bf16[32,64,1,16,8]{0,4,3,1,2:T(8,128)(2,1)S(1)} %copy.37), kind=kOutput, calls=%fused_computation.3 | convolution fusion | flops 20938752 | bytes 5374976 | tf_op jit(solution)/shard_map/tvhd,uvhd->vhtu/dot_general | solution.py:26
  216.4 0.0 copy-done.4
  216.4 9.8 %convert_bitcast_fusion = bf16[32,64,16,8]{0,3,2,1:T(8,128)(2,1)} fusion(f32[64,16,32,32]{2,3,1,0:T(8,128)} %get-tuple-element.9, f32[64,16,32]{2,1,0:T(8,128)S(1)} %get-tuple-element.8, pred[32,32]{0,1:T(8,128)(4,1)S(1)} %iota_compare_fusion, bf16[32,64,1,16,8]{0,4,3,1,2:T(8,128)(2,1)S(1)} %copy-done.4), kind=kOutput, calls=%fused_computation.19 | convolution fusion | flops 22282240 | bytes 5374976 | tf_op jit(solution)/shard_map/vhtu,uvhd->tvhd/dot_general | solution.py:33
  226.1 0.0 copy-start.2
  226.1 0.0 copy-start.6
  226.2 0.0 copy-start.9
  226.2 0.0 copy-start.10
  226.2 3.4 %copy.31 = bf16[32,64,16,8]{1,0,3,2:T(8,128)(2,1)S(1)} copy(bf16[32,64,16,8]{0,3,2,1:T(8,128)(2,1)} %convert_bitcast_fusion) | data formatting | bytes 1048576 | tf_op jit(solution)/shard_map/convert_element_type | solution.py:35
  229.6 0.8 reshape.111
  230.4 0.0 copy-done.2
  230.4 0.0 copy-done.6
  230.4 0.6 fusion.36
  231.0 0.6 multiply_reduce_fusion
  231.6 0.0 copy-done
  231.6 0.0 copy-done.9
  231.7 0.0 copy-done.10
  231.7 1.3 fusion.6
  233.0 12.7 %all_to_all.24 = bf16[32,1,64,128]{3,2,1,0:T(8,128)(2,1)S(1)} all-to-all(bf16[32,1,64,128]{3,2,1,0:T(8,128)(2,1)S(1)} %bitcast.67), channel_id=1, replica_groups=mesh['tm'=8,'vert'=32] {'tm'}, dimensions={0} | all-to-all | bytes 1048576 | tf_op jit(solution)/shard_map/all_to_all | solution.py:89
  245.7 0.8 copy.33
  (5 shorter events, 0.0 us)
Async XLA Ops:
  6.5 225.1 %copy-start = (bf16[512,128]{1,0:T(8,128)(2,1)S(1)}, bf16[512,128]{1,0:T(8,128)(2,1)}, u32[]{:S(2)}) copy-start(bf16[512,128]{1,0:T(8,128)(2,1)} %param.19) | copy-start | bytes 393220
  6.5 146.2 %all-gather.2.cloned.1.call-start = ((), (), s32[]{:S(2)}) async-start(), calls=%async_computation.2 | async-start | bytes 17301504 | tf_op jit(solution)/shard_map/all_gather | solution.py:55
  161.6 4.8 %copy-start.7 = (bf16[128,128]{1,0:T(8,128)(2,1)S(1)}, bf16[128,128]{1,0:T(8,128)(2,1)}, u32[]{:S(2)}) copy-start(bf16[128,128]{1,0:T(8,128)(2,1)} %param.13) | copy-start | bytes 98308
  161.6 11.7 %copy-start.8 = (bf16[32,128]{1,0:T(8,128)(2,1)S(1)}, bf16[32,128]{1,0:T(8,128)(2,1)}, u32[]{:S(2)}) copy-start(bf16[32,128]{1,0:T(8,128)(2,1)} %param.14) | copy-start | bytes 24580
  166.4 17.2 %copy-start.5 = (bf16[128,384]{1,0:T(8,128)(2,1)S(1)}, bf16[128,384]{1,0:T(8,128)(2,1)}, u32[]{:S(2)}) copy-start(bf16[128,384]{1,0:T(8,128)(2,1)} %param.15) | copy-start | bytes 294916
  167.5 15.0 %all-to-all-start = ((bf16[4,8,64,128]{3,2,0,1:T(8,128)(2,1)}), bf16[4,8,64,128]{3,2,0,1:T(8,128)(2,1)S(1)}, u32[]{:S(2)}, u32[]{:S(2)}) async-start(bf16[4,8,64,128]{3,2,0,1:T(8,128)(2,1)} %copy.25), calls=%async_computation | async-start | bytes 1048576 | tf_op jit(solution)/shard_map/all_to_all | solution.py:84
  182.8 0.8 copy-start.1
  192.2 9.1 %copy-start.3 = (bf16[32,64,1,16,8]{1,0,4,3,2:T(8,128)(2,1)S(1)}, bf16[32,64,1,16,8]{1,0,4,3,2:T(8,128)(2,1)}, u32[]{:S(2)}) copy-start(bf16[32,64,1,16,8]{1,0,4,3,2:T(8,128)(2,1)} %get-tuple-element.5) | copy-start | bytes 1572868
  205.2 11.1 %copy-start.4 = (bf16[32,64,1,16,8]{0,4,3,1,2:T(8,128)(2,1)S(1)}, bf16[32,64,1,16,8]{0,4,3,1,2:T(8,128)(2,1)}, u32[]{:S(2)}) copy-start(bf16[32,64,1,16,8]{0,4,3,1,2:T(8,128)(2,1)} %copy.36) | copy-start | bytes 1572868
  226.1 4.2 %copy-start.2 = (bf16[2048,128]{1,0:T(8,128)(2,1)S(1)}, bf16[2048,128]{1,0:T(8,128)(2,1)}, u32[]{:S(2)}) copy-start(bf16[2048,128]{1,0:T(8,128)(2,1)} %copy-done.1) | copy-start | bytes 1572868
  226.1 4.2 %copy-start.6 = (bf16[128,128]{1,0:T(8,128)(2,1)S(1)}, bf16[128,128]{1,0:T(8,128)(2,1)}, u32[]{:S(2)}) copy-start(bf16[128,128]{1,0:T(8,128)(2,1)} %param.16) | copy-start | bytes 98308
  226.2 5.5 %copy-start.9 = (bf16[128,512]{1,0:T(8,128)(2,1)S(1)}, bf16[128,512]{1,0:T(8,128)(2,1)}, u32[]{:S(2)}) copy-start(bf16[128,512]{1,0:T(8,128)(2,1)} %param.18) | copy-start | bytes 393220
  226.2 5.5 %copy-start.10 = (f32[128]{0:T(128)S(1)}, f32[128]{0:T(128)}, u32[]{:S(2)}) copy-start(f32[128]{0:T(128)} %param.17) | copy-start | bytes 1540
Sparse Core Ops, SparseCore 0:
  9.9 142.7 all-gather.1
where the time goes:
time: 254 us; the launch traced here: 253 us
  waiting for transfers between devices  154 us (61%)
  local copies, waits for them, and re-layouts  37.5 us (15%)
  matrix products  28.4 us (11%)
  between operations  13.6 us (5%)
  blocking collectives  12.7 us (5%)
  starting transfers between devices  5.69 us (2%)
    all_gather x1, waiting for transfers between devices, spatial(): everything = lax.all_gather(features, 'vert', axis=1, tiled=True)  144 us
    unnamed x25, local copies, waits for them, and re-layouts  13.9 us
    all_to_all x1, blocking collectives, local(): lax.all_to_all(result, 'tm', split_axis=0, concat_axis=1, tiled=True)  12.7 us
    dot_general x1, matrix products, temporal(): jnp.einsum('tvhd,uvhd->vhtu', query_part, key_part, preferred_element_typ...  11.1 us
    dot_general x1, matrix products, temporal(): jnp.einsum('vhtu,uvhd->tvhd', weights, value_part, preferred_element_type...  9.77 us
    all_to_all x1, waiting for transfers between devices, local(): lax.all_to_all(grouped, 'tm', split_axis=1, concat_axis=0, tiled=True)  9.33 us
    gather x2, local copies, waits for them, and re-layouts, spatial(): jnp.take_along_axis(everything, flat_cols[:, :, None, None], axis=1)  8.93 us
    all_to_all x1, starting transfers between devices, local(): lax.all_to_all(grouped, 'tm', split_axis=1, concat_axis=0, tiled=True)  5.69 us
  transfers between devices with their start and end apart: 2, of which 2 were waited for; matrix products, arithmetic and copies ran while one was open for 1% of the time, Pallas kernels for 0%

commit v1 on v0

--- a/solution.py
+++ b/solution.py
@@ -52,7 +52,9 @@
     block_count = row_count // tile_size
     tile_count = tile_cols.shape[2]
     flat_cols = tile_cols.reshape(snap_count, block_count * tile_count)
-    everything = lax.all_gather(features, "vert", axis=1, tiled=True)
+    everything = jnp.concatenate(
+        lax.all_to_all(jnp.stack([features] * lax.axis_size("vert")), "vert", 0, 0), axis=1
+    )
     everything = everything.reshape(snap_count, -1, tile_size, feature_dim)
     blocks = jnp.take_along_axis(everything, flat_cols[:, :, None, None], axis=1)
     blocks = blocks.reshape(snap_count, block_count, tile_count, tile_size, feature_dim)

time: 254 us -> 534 us (2.10)
  the two profiles are of different devices: /device:TPU:1 before, /device:TPU:4 now
where the time goes in v1:
time: 534 us; the launch traced here: 533 us
  waiting for transfers between devices  417 us (78%)
  local copies, waits for them, and re-layouts  57.8 us (11%)
  matrix products  28.4 us (5%)
  starting transfers between devices  16.3 us (3%)
  blocking collectives  12.8 us (2%)
    all_to_all x1, waiting for transfers between devices, spatial(): lax.all_to_all(jnp.stack([features] * lax.axis_size('vert')), 'vert', 0, 0)  407 us
    all_to_all x1, local copies, waits for them, and re-layouts, spatial(): lax.all_to_all(jnp.stack([features] * lax.axis_size('vert')), 'vert', 0, 0)  13.9 us
    unnamed x27, local copies, waits for them, and re-layouts  13.9 us
    all_to_all x1, blocking collectives, local(): lax.all_to_all(result, 'tm', split_axis=0, concat_axis=1, tiled=True)  12.8 us
    all_to_all x1, starting transfers between devices, spatial(): lax.all_to_all(jnp.stack([features] * lax.axis_size('vert')), 'vert', 0, 0)  11.8 us
    dot_general x1, matrix products, temporal(): jnp.einsum('tvhd,uvhd->vhtu', query_part, key_part, preferred_element_typ...  11.1 us
  transfers between devices with their start and end apart: 2, of which 2 were waited for; matrix products, arithmetic and copies ran while one was open for 0% of the time, Pallas kernels for 0%

profile of v1, /device:TPU:4, one launch (start us, length us, event | category | flops | bytes accessed | tf_op | source)
XLA Modules:
  0.0 533.1 jit_solution(11694064284142756954)
XLA Ops:
  0.0 0.0 copy-start
  0.0 7.1 %stack.2 = bf16[32,4,512,128]{3,2,1,0:T(8,128)(2,1)} broadcast(bf16[4,512,128]{2,1,0:T(8,128)(2,1)} %param.10), dimensions={1,2,3} | broadcast | bytes 17301504 | tf_op jit(solution)/shard_map/stack | solution.py:56
  7.1 0.0 copy-start.8
  7.1 11.8 %all-to-all-start = ((bf16[32,4,512,128]{3,2,1,0:T(8,128)(2,1)}), bf16[32,4,512,128]{3,2,1,0:T(8,128)(2,1)}, u32[]{:S(2)}, u32[]{:S(2)}) async-start(bf16[32,4,512,128]{3,2,1,0:T(8,128)(2,1)} %stack.2), calls=%async_computation | async-start | bytes 33554432 | tf_op jit(solution)/shard_map/all_to_all | solution.py:56
  18.8 0.0 copy-done.8
  18.9 0.1 broadcast_in_dim_reshape.3
  18.9 0.1 reshape.117
  19.1 406.5 %all-to-all-done = bf16[32,4,512,128]{3,2,1,0:T(8,128)(2,1)} async-done(((bf16[32,4,512,128]{3,2,1,0:T(8,128)(2,1)}), bf16[32,4,512,128]{3,2,1,0:T(8,128)(2,1)}, u32[]{:S(2)}, u32[]{:S(2)}) %all-to-all-start) | async-done | bytes 16777248 | tf_op jit(solution)/shard_map/all_to_all | solution.py:56
  425.6 13.9 %copy.25 = bf16[32,4,512,128]{3,2,0,1:T(8,128)(2,1)} copy(bf16[32,4,512,128]{3,2,1,0:T(8,128)(2,1)} %all-to-all-done) | data formatting | bytes 33554432 | tf_op jit(solution)/shard_map/all_to_all | solution.py:56
  439.5 8.8 %gather_fusion = bf16[128,128,128]{2,1,0:T(8,128)(2,1)} fusion(bf16[4,128,128,128]{3,2,1,0:T(8,128)(2,1)} %bitcast.65, s32[128]{0:T(128)S(1)} %reshape.117), kind=kCustom, calls=%fused_computation | custom fusion | bytes 8389632 | tf_op jit(solution)/shard_map/jit(take_along_axis)/gather | solution.py:59
  448.4 0.0 copy-start.7
  448.4 0.0 copy-start.9
  448.4 4.8 fusion.17
  453.2 0.0 copy-start.5
  453.2 0.0 copy-done.7
  453.2 0.3 fusion.5
  453.5 0.8 copy.26
  454.3 4.5 all-to-all-start.1
  458.8 0.0 copy-done.9
  458.8 10.3 %all-to-all-done.1 = bf16[4,8,64,128]{3,2,0,1:T(8,128)(2,1)S(1)} async-done(((bf16[4,8,64,128]{3,2,0,1:T(8,128)(2,1)}), bf16[4,8,64,128]{3,2,0,1:T(8,128)(2,1)S(1)}, u32[]{:S(2)}, u32[]{:S(2)}) %all-to-all-start.1) | async-done | bytes 524320 | tf_op jit(solution)/shard_map/all_to_all | solution.py:86
  469.1 0.1 bitcast_convert_fusion
  469.2 0.1 fusion.20
  469.3 0.0 copy-start.1
  469.3 0.8 copy-done.1
  470.1 0.0 copy-done.5
  470.1 0.6 convolution_convert_fusion
  470.7 1.7 copy.27
  472.4 4.6 reshape.112
  476.9 1.8 fusion.35
  478.7 0.0 copy-start.3
  478.7 4.3 copy.38
  483.0 4.9 copy.39
  487.9 0.0 copy-done.3
  487.9 3.9 copy.37
  491.8 0.0 copy-start.4
  491.8 11.1 %fusion = (f32[64,16,32]{2,1,0:T(8,128)S(1)}, f32[64,16,32,32]{2,3,1,0:T(8,128)}) fusion(pred[32,32]{0,1:T(8,128)(4,1)S(1)} %iota_compare_fusion, bf16[32,64,1,16,8]{0,4,3,1,2:T(8,128)(2,1)} %copy.39, bf16[32,64,1,16,8]{0,4,3,1,2:T(8,128)(2,1)S(1)} %copy.38), kind=kOutput, calls=%fused_computation.3 | convolution fusion | flops 20938752 | bytes 5374976 | tf_op jit(solution)/shard_map/tvhd,uvhd->vhtu/dot_general | solution.py:26
  502.9 0.0 copy-done.4
  502.9 9.8 %convert_bitcast_fusion = bf16[32,64,16,8]{0,3,2,1:T(8,128)(2,1)} fusion(f32[64,16,32,32]{2,3,1,0:T(8,128)} %get-tuple-element.9, f32[64,16,32]{2,1,0:T(8,128)S(1)} %get-tuple-element.8, pred[32,32]{0,1:T(8,128)(4,1)S(1)} %iota_compare_fusion, bf16[32,64,1,16,8]{0,4,3,1,2:T(8,128)(2,1)S(1)} %copy-done.4), kind=kOutput, calls=%fused_computation.19 | convolution fusion | flops 22282240 | bytes 5374976 | tf_op jit(solution)/shard_map/vhtu,uvhd->tvhd/dot_general | solution.py:33
  512.7 0.0 copy-start.2
  512.7 0.0 copy-start.6
  512.7 0.0 copy-start.10
  512.7 0.0 copy-start.11
  512.7 3.4 copy.32
  516.1 0.8 reshape.113
  516.9 0.0 copy-done.2
  516.9 0.0 copy-done.6
  517.0 0.6 fusion.36
  517.5 0.6 multiply_reduce_fusion
  518.2 0.0 copy-done
  518.2 0.0 copy-done.10
  518.2 0.0 copy-done.11
  518.2 1.3 fusion.6
  519.5 12.8 %all_to_all.29 = bf16[32,1,64,128]{3,2,1,0:T(8,128)(2,1)S(1)} all-to-all(bf16[32,1,64,128]{3,2,1,0:T(8,128)(2,1)S(1)} %bitcast.69), channel_id=1, replica_groups=mesh['tm'=8,'vert'=32] {'tm'}, dimensions={0} | all-to-all | bytes 1048576 | tf_op jit(solution)/shard_map/all_to_all | solution.py:91
  532.3 0.8 copy.34
  (6 shorter events, 0.0 us)
Async XLA Ops:
  0.0 518.2 %copy-start = (bf16[512,128]{1,0:T(8,128)(2,1)S(1)}, bf16[512,128]{1,0:T(8,128)(2,1)}, u32[]{:S(2)}) copy-start(bf16[512,128]{1,0:T(8,128)(2,1)} %param.19) | copy-start | bytes 393220
  7.1 11.8 %copy-start.8 = (s32[4,4,8]{2,1,0:T(4,128)S(1)}, s32[4,4,8]{2,1,0:T(4,128)}, u32[]{:S(2)}) copy-start(s32[4,4,8]{2,1,0:T(4,128)} %param.11) | copy-start | bytes 1540
  7.1 418.5 %all-to-all-start = ((bf16[32,4,512,128]{3,2,1,0:T(8,128)(2,1)}), bf16[32,4,512,128]{3,2,1,0:T(8,128)(2,1)}, u32[]{:S(2)}, u32[]{:S(2)}) async-start(bf16[32,4,512,128]{3,2,1,0:T(8,128)(2,1)} %stack.2), calls=%async_computation | async-start | bytes 33554432 | tf_op jit(solution)/shard_map/all_to_all | solution.py:56
  448.4 4.8 copy-start.7
  448.4 10.4 %copy-start.9 = (bf16[32,128]{1,0:T(8,128)(2,1)S(1)}, bf16[32,128]{1,0:T(8,128)(2,1)}, u32[]{:S(2)}) copy-start(bf16[32,128]{1,0:T(8,128)(2,1)} %param.14) | copy-start | bytes 24580
  453.2 16.9 %copy-start.5 = (bf16[128,384]{1,0:T(8,128)(2,1)S(1)}, bf16[128,384]{1,0:T(8,128)(2,1)}, u32[]{:S(2)}) copy-start(bf16[128,384]{1,0:T(8,128)(2,1)} %param.15) | copy-start | bytes 294916
  454.3 14.8 %all-to-all-start.1 = ((bf16[4,8,64,128]{3,2,0,1:T(8,128)(2,1)}), bf16[4,8,64,128]{3,2,0,1:T(8,128)(2,1)S(1)}, u32[]{:S(2)}, u32[]{:S(2)}) async-start(bf16[4,8,64,128]{3,2,0,1:T(8,128)(2,1)} %copy.26), calls=%async_computation.1 | async-start | bytes 1048576 | tf_op jit(solution)/shard_map/all_to_all | solution.py:86
  469.3 0.8 copy-start.1
  478.7 9.1 %copy-start.3 = (bf16[32,64,1,16,8]{1,0,4,3,2:T(8,128)(2,1)S(1)}, bf16[32,64,1,16,8]{1,0,4,3,2:T(8,128)(2,1)}, u32[]{:S(2)}) copy-start(bf16[32,64,1,16,8]{1,0,4,3,2:T(8,128)(2,1)} %get-tuple-element.5) | copy-start | bytes 1572868
  491.8 11.1 %copy-start.4 = (bf16[32,64,1,16,8]{0,4,3,1,2:T(8,128)(2,1)S(1)}, bf16[32,64,1,16,8]{0,4,3,1,2:T(8,128)(2,1)}, u32[]{:S(2)}) copy-start(bf16[32,64,1,16,8]{0,4,3,1,2:T(8,128)(2,1)} %copy.37) | copy-start | bytes 1572868
  512.7 4.2 copy-start.2
  512.7 4.2 copy-start.6
  512.7 5.5 %copy-start.10 = (bf16[128,512]{1,0:T(8,128)(2,1)S(1)}, bf16[128,512]{1,0:T(8,128)(2,1)}, u32[]{:S(2)}) copy-start(bf16[128,512]{1,0:T(8,128)(2,1)} %param.18) | copy-start | bytes 393220
  512.7 5.5 %copy-start.11 = (f32[128]{0:T(128)S(1)}, f32[128]{0:T(128)}, u32[]{:S(2)}) copy-start(f32[128]{0:T(128)} %param.17) | copy-start | bytes 1540
